TPU v7x, 32 devices: a whole 2x2x4 slice. The times are simulated.
32 devices in a mesh: imp: 8 (over z, y), camp: 4 (over x, core).
Axes of the slice: x: 2, y: 2, z: 4, core: 2. Of those that a mesh axis runs over, the one named last changes fastest.
Arguments:
- imp_emb: bfloat16 [16384, 256], P(('imp', 'camp')), may hold values from -512 to 512
- imp_cost: bfloat16 [16384], P(('imp', 'camp')), may hold values from 0.099609375 to 1
- camp_emb: bfloat16 [4096, 256], P(('camp', 'imp')), may hold values from -6 to 6
- prices: bfloat16 [4096], P(('camp', 'imp')), may hold values from -5 to 5
- spend_limits: float32 [4096], P(('camp', 'imp')), may hold values from 3 to 32
- block_lists: int32 [128, 4, 8], P('imp', 'camp'), may hold values from 0 to 7, as said below
- block_counts: int32 [128, 4], P('imp', 'camp'), may hold values from 1 to 8, as said below
Outputs:
- new_prices: float32 [4096], P(('camp', 'imp'))
- row_logz: float32 [16384], P('imp')
Inputs may be any that keep to these rules, and one draw needn't show every extreme that they name: `block_lists`: entries of a list of one tile and owner are distinct block numbers of that owner; slots past the count hold block numbers too, which are ignored. `block_counts`: tile 0 uses all 8 slots of every owner.
All inputs are finite; a program needn't handle non-finite values.
Results may differ from a plain program's by a relative error of at most 0.0003.
Values may be sent and summed in bfloat16 or wider, within the bound.
A program may use at most 64 MiB of HBM per device.

v0:
```python
import jax
import jax.numpy as jnp
from jax import lax
from jax.sharding import PartitionSpec as P

D = 256
BLOCK = 128
SLOTS = 8
GROUP = 4


def merged(array, axis, combine):
    everything = jax.tree.map(lambda part: lax.all_gather(part, axis), array)
    initial = jax.tree.map(lambda part: part[0], everything)

    def step(k, so_far):
        return combine(so_far, jax.tree.map(lambda part: part[k], everything))

    return lax.fori_loop(1, lax.axis_size(axis), step, initial)


def local(imp_emb, imp_cost, camp_emb, prices, spend_limits, block_lists, block_counts):
    scale = 3.0 / jnp.sqrt(jnp.float32(D))
    emb_rows, cost_rows = (
        lax.all_gather(imp_emb, "camp", axis=0, tiled=True),
        lax.all_gather(imp_cost, "camp", axis=0, tiled=True),
    )
    camp_all, price_all = (
        lax.all_gather(camp_emb, "imp", axis=0, tiled=True),
        lax.all_gather(prices, "imp", axis=0, tiled=True),
    )
    own_count = camp_all.shape[0] // BLOCK
    camp_table = camp_all.reshape(own_count, BLOCK, D)
    price_table = price_all.astype(jnp.float32).reshape(own_count, BLOCK)
    lists = block_lists[:, 0, :]
    counts = block_counts[:, 0]
    tiles = lists.shape[0]
    turns = tiles // GROUP
    emb_groups = emb_rows.reshape(turns, GROUP, BLOCK, D)
    cost_groups = cost_rows.astype(jnp.float32).reshape(turns, GROUP, BLOCK)
    list_groups = lists.reshape(turns, GROUP, SLOTS)
    count_groups = counts.reshape(turns, GROUP)

    def scores_of(emb, ids, cnt):
        chosen = camp_table[ids]
        chosen_price = price_table[ids]
        raw = jnp.einsum("gbd,gscd->gbsc", emb, chosen, preferred_element_type=jnp.float32)
        logits = raw * scale - chosen_price[:, None, :, :]
        live = (jnp.arange(SLOTS, dtype=jnp.int32)[None, :] < cnt[:, None])[:, None, :, None]
        return (logits, live)

    def local_both(items):
        emb, ids, cnt = items
        logits, live = scores_of(emb, ids, cnt)
        top_here = jnp.max(jnp.where(live, logits, -jnp.inf), axis=(2, 3))
        expo = jnp.exp(jnp.where(live, logits - top_here[:, :, None, None], -jnp.inf))
        return (top_here, jnp.sum(expo, axis=(2, 3)))

    tops_here, totals_here = lax.map(local_both, (emb_groups, list_groups, count_groups))

    def combine(first, second):
        larger = jnp.maximum(first[0], second[0])
        summed = first[1] * jnp.exp(first[0] - larger) + second[1] * jnp.exp(second[0] - larger)
        return (larger, summed)

    top, total = merged((tops_here, totals_here), "camp", combine)
    row_logz = (top + jnp.log(total)).reshape(tiles * BLOCK)
    block_index = jnp.arange(own_count, dtype=jnp.int32)

    def accumulate(spend, items):
        emb, ids, cnt, cost, top_now, total_now = items
        logits, live = scores_of(emb, ids, cnt)
        expo = jnp.exp(jnp.where(live, logits - top_now[:, :, None, None], -jnp.inf))
        weight = expo / total_now[:, :, None, None]
        contrib = jnp.sum(weight * cost[:, :, None, None], axis=1)
        slot_live = jnp.arange(SLOTS, dtype=jnp.int32)[None, :] < cnt[:, None]
        onehot = ((ids[:, :, None] == block_index[None, None, :]) & slot_live[:, :, None]).astype(
            jnp.float32
        )
        added = jnp.einsum("gso,gsc->oc", onehot, contrib, precision=lax.Precision.HIGHEST)
        return (spend + added, None)

    spend_zero = jnp.zeros((own_count, BLOCK), jnp.float32)
    spend, unused = lax.scan(
        accumulate, spend_zero, (emb_groups, list_groups, count_groups, cost_groups, top, total)
    )
    spend = spend.reshape(own_count * BLOCK)
    width = prices.shape[0]
    whole = lax.psum(spend, "imp")
    mine = lax.dynamic_slice_in_dim(whole, lax.axis_index("imp") * width, width)
    new_prices = prices.astype(jnp.float32) + 2.0 * (mine - spend_limits) / (mine + spend_limits)
    return (new_prices, row_logz)


def solution(mesh):
    return jax.shard_map(
        local,
        mesh=mesh,
        in_specs=(
            P(("imp", "camp"), None),
            P(("imp", "camp")),
            P(("camp", "imp"), None),
            P(("camp", "imp")),
            P(("camp", "imp")),
            P("imp", "camp", None),
            P("imp", "camp"),
        ),
        out_specs=(P(("camp", "imp")), P("imp")),
        check_vma=False,
    )
```

profile of v0, /device:TPU:0, one launch (start us, length us, event | category | flops | bytes accessed | tf_op | source)
XLA Modules:
  0.0 137.3 jit_solution(15288913521605371296)
XLA Ops:
  7.9 0.8 copy.12
  8.7 22.5 %all-gather.2 = bf16[8,1,128]{2,1,0:T(2,128)(2,1)S(1)} all-gather(bf16[1,1,128]{2,1,0:T(2,128)(2,1)} %bitcast.128), channel_id=1, replica_groups=mesh['imp'=8,'camp'=4] {'imp'}, dimensions={0}, use_global_device_ids=true | all-gather | bytes 2304 | tf_op jit(solution)/shard_map/all_gather | solution.py:30
  31.7 1.2 reduce.3
  33.7 5.2 %all-gather.3 = bf16[4,1,512]{2,1,0:T(2,128)(2,1)S(1)} all-gather(bf16[1,1,512]{2,1,0:T(2,128)(2,1)S(1)} %reshape.223), channel_id=1, replica_groups=mesh['imp'=8,'camp'=4] {'camp'}, dimensions={0}, use_global_device_ids=true | all-gather | bytes 5120 | tf_op jit(solution)/shard_map/all_gather | solution.py:26
  38.9 31.4 %all_gather.25 = bf16[1024,256]{1,0:T(8,128)(2,1)S(1)} all-gather(bf16[128,256]{1,0:T(8,128)(2,1)} %param.15), channel_id=1, replica_groups=mesh['imp'=8,'camp'=4] {'imp'}, dimensions={0}, use_global_device_ids=true | all-gather | bytes 589824 | tf_op jit(solution)/shard_map/all_gather | solution.py:29
  70.3 16.5 %while.40 = (s32[]{:T(128)}, f32[4,4,128]{2,1,0:T(4,128)S(1)}, f32[4,4,128]{2,1,0:T(4,128)S(1)}, s32[4,4]{1,0:T(4,128)S(1)}, bf16[4,4,128,256]{3,2,1,0:T(8,128)(...) while((s32[]{:T(128)}, f32[4,4,128]{2,1,0:T(4,128)S(1)}, ...), condition=%wide.region_3.4_spmd, body=%wide.region_0.3_spmd.sunk | while | flops 273154176 | bytes 10833529 | solution.py:59
  71.7 1.9 %select_reduce_fusion.2 = (f32[4,128]{1,0:T(4,128)S(1)}, f32[4,128,8,128]{1,3,2,0:T(8,128)S(1)}) fusion(f32[4,8,128]{2,1,0:T(8,128)S(1)} %bitcast.117, pred[4,8]{1,0:T(4,128)(4,1)S(1)} %iota_compare_fusion.5, bf16[4,8,128,256]{3,2,1,0:T(8,128)(2,1)S(1)} %bitcast.116, bf16[4,4,128,256]{3,2,1,0:T(8,128)(2,1)} %get-tuple-element.508, ...), kind=kOutput, calls=%fused_computation.11.clone.1 | convolution fusion | flops 270532096 | bytes 4475424 | tf_op jit(solution)/shard_map/while/body/eval_jaxpr/gbd,gscd->gbsc/dot_general | solution.py:47
  73.6 0.8 exponential_reduce_fusion.2
  75.9 1.9 %select_reduce_fusion.2 = (f32[4,128]{1,0:T(4,128)S(1)}, f32[4,128,8,128]{1,3,2,0:T(8,128)S(1)}) fusion(f32[4,8,128]{2,1,0:T(8,128)S(1)} %bitcast.117, pred[4,8]{1,0:T(4,128)(4,1)S(1)} %iota_compare_fusion.5, bf16[4,8,128,256]{3,2,1,0:T(8,128)(2,1)S(1)} %bitcast.116, bf16[4,4,128,256]{3,2,1,0:T(8,128)(2,1)} %get-tuple-element.508, ...), kind=kOutput, calls=%fused_computation.11.clone.1 | convolution fusion | flops 270532096 | bytes 4475424 | tf_op jit(solution)/shard_map/while/body/eval_jaxpr/gbd,gscd->gbsc/dot_general | solution.py:47
  77.7 0.8 exponential_reduce_fusion.2
  80.0 1.9 %select_reduce_fusion.2 = (f32[4,128]{1,0:T(4,128)S(1)}, f32[4,128,8,128]{1,3,2,0:T(8,128)S(1)}) fusion(f32[4,8,128]{2,1,0:T(8,128)S(1)} %bitcast.117, pred[4,8]{1,0:T(4,128)(4,1)S(1)} %iota_compare_fusion.5, bf16[4,8,128,256]{3,2,1,0:T(8,128)(2,1)S(1)} %bitcast.116, bf16[4,4,128,256]{3,2,1,0:T(8,128)(2,1)} %get-tuple-element.508, ...), kind=kOutput, calls=%fused_computation.11.clone.1 | convolution fusion | flops 270532096 | bytes 4475424 | tf_op jit(solution)/shard_map/while/body/eval_jaxpr/gbd,gscd->gbsc/dot_general | solution.py:47
  81.9 0.8 exponential_reduce_fusion.2
  84.1 1.9 %select_reduce_fusion.2 = (f32[4,128]{1,0:T(4,128)S(1)}, f32[4,128,8,128]{1,3,2,0:T(8,128)S(1)}) fusion(f32[4,8,128]{2,1,0:T(8,128)S(1)} %bitcast.117, pred[4,8]{1,0:T(4,128)(4,1)S(1)} %iota_compare_fusion.5, bf16[4,8,128,256]{3,2,1,0:T(8,128)(2,1)S(1)} %bitcast.116, bf16[4,4,128,256]{3,2,1,0:T(8,128)(2,1)} %get-tuple-element.508, ...), kind=kOutput, calls=%fused_computation.11.clone.1 | convolution fusion | flops 270532096 | bytes 4475424 | tf_op jit(solution)/shard_map/while/body/eval_jaxpr/gbd,gscd->gbsc/dot_general | solution.py:47
  86.0 0.8 exponential_reduce_fusion.2
  86.8 5.2 %all-gather = f32[16,4,128]{2,1,0:T(4,128)S(1)} all-gather(f32[4,4,128]{2,1,0:T(4,128)S(1)} %get-tuple-element.235), channel_id=2, replica_groups=mesh['imp'=8,'camp'=4] {'camp'}, dimensions={0}, use_global_device_ids=true | all-gather | bytes 40960 | tf_op jit(solution)/shard_map/all_gather | solution.py:13
  92.0 5.2 %all-gather.1 = f32[16,4,128]{2,1,0:T(4,128)S(1)} all-gather(f32[4,4,128]{2,1,0:T(4,128)S(1)} %get-tuple-element.236), channel_id=3, replica_groups=mesh['imp'=8,'camp'=4] {'camp'}, dimensions={0}, use_global_device_ids=true | all-gather | bytes 40960 | tf_op jit(solution)/shard_map/all_gather | solution.py:13
  97.3 14.7 %while.42 = (s32[]{:T(128)}, f32[8,128]{1,0:T(8,128)S(1)}, s32[4,4,8]{2,1,0:T(4,128)S(1)}, s32[4,4]{1,0:T(4,128)S(1)}, bf16[4,4,128,256]{3,2,1,0:T(8,128)(2,1)},...) while((s32[]{:T(128)}, f32[8,128]{1,0:T(8,128)S(1)}, ...), condition=%wide.region_8.9_spmd.clone, body=%wide.region_6.8_spmd.clone.sunk | while | flops 272498304 | bytes 6668323 | solution.py:84
  98.8 2.0 %multiply_reduce_fusion.2 = f32[4,8,128]{2,1,0:T(8,128)S(1)} fusion(bf16[4,8,128,256]{3,2,1,0:T(8,128)(2,1)S(1)} %bitcast.115, f32[4,128]{1,0:T(4,128)S(1)} %get-tuple-element.484, f32[4,128]{1,0:T(4,128)S(1)} %get-tuple-element.485, f32[4,128]{1,0:T(4,128)S(1)} %dynamic-slice_bitcast_fusion.8, f32[4,8,128]{2,1,0:T(8,128)S(1)} %bitcast.121, ...), kind=kOutput, calls=%fused_computation.24.clone.1 | convolution fusion | flops 272101376 | bytes 2398752 | tf_op jit(solution)/shard_map/while/body/eval_jaxpr/gbd,gscd->gbsc/dot_general | solution.py:47
  101.1 0.7 gather_fusion.2
  102.5 2.0 %multiply_reduce_fusion.2 = f32[4,8,128]{2,1,0:T(8,128)S(1)} fusion(bf16[4,8,128,256]{3,2,1,0:T(8,128)(2,1)S(1)} %bitcast.115, f32[4,128]{1,0:T(4,128)S(1)} %get-tuple-element.484, f32[4,128]{1,0:T(4,128)S(1)} %get-tuple-element.485, f32[4,128]{1,0:T(4,128)S(1)} %dynamic-slice_bitcast_fusion.8, f32[4,8,128]{2,1,0:T(8,128)S(1)} %bitcast.121, ...), kind=kOutput, calls=%fused_computation.24.clone.1 | convolution fusion | flops 272101376 | bytes 2398752 | tf_op jit(solution)/shard_map/while/body/eval_jaxpr/gbd,gscd->gbsc/dot_general | solution.py:47
  104.8 0.7 gather_fusion.2
  106.2 2.0 %multiply_reduce_fusion.2 = f32[4,8,128]{2,1,0:T(8,128)S(1)} fusion(bf16[4,8,128,256]{3,2,1,0:T(8,128)(2,1)S(1)} %bitcast.115, f32[4,128]{1,0:T(4,128)S(1)} %get-tuple-element.484, f32[4,128]{1,0:T(4,128)S(1)} %get-tuple-element.485, f32[4,128]{1,0:T(4,128)S(1)} %dynamic-slice_bitcast_fusion.8, f32[4,8,128]{2,1,0:T(8,128)S(1)} %bitcast.121, ...), kind=kOutput, calls=%fused_computation.24.clone.1 | convolution fusion | flops 272101376 | bytes 2398752 | tf_op jit(solution)/shard_map/while/body/eval_jaxpr/gbd,gscd->gbsc/dot_general | solution.py:47
  109.9 2.0 %multiply_reduce_fusion.2 = f32[4,8,128]{2,1,0:T(8,128)S(1)} fusion(bf16[4,8,128,256]{3,2,1,0:T(8,128)(2,1)S(1)} %bitcast.115, f32[4,128]{1,0:T(4,128)S(1)} %get-tuple-element.484, f32[4,128]{1,0:T(4,128)S(1)} %get-tuple-element.485, f32[4,128]{1,0:T(4,128)S(1)} %dynamic-slice_bitcast_fusion.8, f32[4,8,128]{2,1,0:T(8,128)S(1)} %bitcast.121, ...), kind=kOutput, calls=%fused_computation.24.clone.1 | convolution fusion | flops 272101376 | bytes 2398752 | tf_op jit(solution)/shard_map/while/body/eval_jaxpr/gbd,gscd->gbsc/dot_general | solution.py:47
  112.1 17.2 %psum.7 = f32[1024]{0:T(1024)S(1)} all-reduce(f32[1024]{0:T(1024)S(1)} %bitcast.125), channel_id=1, replica_groups=mesh['imp'=8,'camp'=4] {'imp'}, use_global_device_ids=true, to_apply=%region_9.10 | all-reduce | flops 1024 | bytes 8192 | tf_op jit(solution)/shard_map/psum | solution.py:89
  (97 shorter events, 14.5 us)
Async XLA Ops:
  7.2 63.1 %all-gather.6.cloned.1.call-start = ((), (), s32[]{:S(2)}) async-start(), calls=%async_computation | async-start | bytes 1310720 | tf_op jit(solution)/shard_map/all_gather | solution.py:25
  97.3 32.6 %copy-start = (bf16[128]{0:T(256)(128)(2,1)S(1)}, bf16[128]{0:T(256)(128)(2,1)}, u32[]{:S(2)}) copy-start(bf16[128]{0:T(256)(128)(2,1)} %param.16) | copy-start | bytes 772
  97.3 32.6 %copy-start.1 = (f32[128]{0:T(128)S(1)}, f32[128]{0:T(128)}, u32[]{:S(2)}) copy-start(f32[128]{0:T(128)} %param.17) | copy-start | bytes 1540
Sparse Core Ops, SparseCore 0:
  9.5 19.4 all-gather.5
where the time goes:
time: 138 us; the launch traced here: 137 us
  blocking collectives  86.6 us (63%)
  matrix products  16 us (12%)
  between operations  14.1 us (10%)
  local copies, waits for them, and re-layouts  13 us (9%)
  other arithmetic  6.35 us (5%)
    all_gather x1, blocking collectives, local(): lax.all_gather(camp_emb, 'imp', axis=0, tiled=True)  31.4 us
    all_gather x1, blocking collectives, local(): lax.all_gather(prices, 'imp', axis=0, tiled=True)  22.5 us
    psum x1, blocking collectives, local(): whole = lax.psum(spend, 'imp')  17.2 us
    dot_general x8, matrix products, scores_of(): jnp.einsum('gbd,gscd->gbsc', emb, chosen, preferred_element_type=jnp.floa...  15.3 us
    all_gather x2, blocking collectives, merged(): everything = jax.tree.map(lambda part: lax.all_gather(part, axis), array)  10.4 us
    gather x8, local copies, waits for them, and re-layouts, scores_of(): chosen = camp_table[ids]  5.48 us
    all_gather x1, blocking collectives, local(): lax.all_gather(imp_cost, 'camp', axis=0, tiled=True)  5.18 us
    gather x8, local copies, waits for them, and re-layouts, scores_of(): chosen_price = price_table[ids]  4.59 us
  transfers between devices with their start and end apart: 1, of which 0 were waited for; matrix products, arithmetic and copies ran while one was open for 2% of the time, Pallas kernels for 0%

commit v1 on v0

--- a/solution.py
+++ b/solution.py
@@ -86,7 +86,7 @@
     )
     spend = spend.reshape(own_count * BLOCK)
     width = prices.shape[0]
-    whole = lax.psum(spend, "imp")
+    whole = lax.all_gather(spend, "imp").sum(axis=0)
     mine = lax.dynamic_slice_in_dim(whole, lax.axis_index("imp") * width, width)
     new_prices = prices.astype(jnp.float32) + 2.0 * (mine - spend_limits) / (mine + spend_limits)
     return (new_prices, row_logz)

time: 138 us -> 151 us (1.094)
  blocking collectives: 86.6 us -> 100 us
    all_gather x0 -> x1, blocking collectives: none -> 30.6 us  [local(): whole = lax.all_gather(spend, 'imp').sum(axis=0)]
    psum x1 -> x0, blocking collectives: 17.2 us -> none  [local(): whole = lax.psum(spend, 'imp')]
where the time goes in v1:
time: 151 us
  blocking collectives  100 us (66%)
  matrix products  16 us (11%)
  between operations  14.1 us (9%)
  local copies, waits for them, and re-layouts  13 us (9%)
  other arithmetic  6.38 us (4%)
    all_gather x1, blocking collectives, local(): lax.all_gather(camp_emb, 'imp', axis=0, tiled=True)  31.4 us
    all_gather x1, blocking collectives, local(): whole = lax.all_gather(spend, 'imp').sum(axis=0)  30.6 us
    all_gather x1, blocking collectives, local(): lax.all_gather(prices, 'imp', axis=0, tiled=True)  22.5 us
    dot_general x8, matrix products, scores_of(): jnp.einsum('gbd,gscd->gbsc', emb, chosen, preferred_element_type=jnp.floa...  15.3 us
    all_gather x2, blocking collectives, merged(): everything = jax.tree.map(lambda part: lax.all_gather(part, axis), array)  10.4 us
    gather x8, local copies, waits for them, and re-layouts, scores_of(): chosen = camp_table[ids]  5.48 us
    all_gather x1, blocking collectives, local(): lax.all_gather(imp_cost, 'camp', axis=0, tiled=True)  5.18 us
    gather x8, local copies, waits for them, and re-layouts, scores_of(): chosen_price = price_table[ids]  4.59 us
  transfers between devices with their start and end apart: 1, of which 0 were waited for; matrix products, arithmetic and copies ran while one was open for 2% of the time, Pallas kernels for 0%

profile of v1, /device:TPU:0, one launch (start us, length us, event | category | flops | bytes accessed | tf_op | source)
XLA Modules:
  0.0 150.8 jit_solution(18296649234135133418)
XLA Ops:
  7.9 0.8 copy.12
  8.7 22.5 %all-gather.2 = bf16[8,1,128]{2,1,0:T(2,128)(2,1)S(1)} all-gather(bf16[1,1,128]{2,1,0:T(2,128)(2,1)} %bitcast.128), channel_id=1, replica_groups=mesh['imp'=8,'camp'=4] {'imp'}, dimensions={0}, use_global_device_ids=true | all-gather | bytes 2304 | tf_op jit(solution)/shard_map/all_gather | solution.py:30
  31.7 1.2 reduce.4
  33.7 5.2 %all-gather.3 = bf16[4,1,512]{2,1,0:T(2,128)(2,1)S(1)} all-gather(bf16[1,1,512]{2,1,0:T(2,128)(2,1)S(1)} %reshape.219), channel_id=1, replica_groups=mesh['imp'=8,'camp'=4] {'camp'}, dimensions={0}, use_global_device_ids=true | all-gather | bytes 5120 | tf_op jit(solution)/shard_map/all_gather | solution.py:26
  38.9 31.4 %all_gather.28 = bf16[1024,256]{1,0:T(8,128)(2,1)S(1)} all-gather(bf16[128,256]{1,0:T(8,128)(2,1)} %param.15), channel_id=1, replica_groups=mesh['imp'=8,'camp'=4] {'imp'}, dimensions={0}, use_global_device_ids=true | all-gather | bytes 589824 | tf_op jit(solution)/shard_map/all_gather | solution.py:29
  70.3 16.5 %while.40 = (s32[]{:T(128)}, f32[4,4,128]{2,1,0:T(4,128)S(1)}, f32[4,4,128]{2,1,0:T(4,128)S(1)}, s32[4,4]{1,0:T(4,128)S(1)}, bf16[4,4,128,256]{3,2,1,0:T(8,128)(...) while((s32[]{:T(128)}, f32[4,4,128]{2,1,0:T(4,128)S(1)}, ...), condition=%wide.region_3.4_spmd, body=%wide.region_0.3_spmd.sunk | while | flops 273154176 | bytes 10833529 | solution.py:59
  71.7 1.9 %select_reduce_fusion.2 = (f32[4,128]{1,0:T(4,128)S(1)}, f32[4,128,8,128]{1,3,2,0:T(8,128)S(1)}) fusion(f32[4,8,128]{2,1,0:T(8,128)S(1)} %bitcast.117, pred[4,8]{1,0:T(4,128)(4,1)S(1)} %iota_compare_fusion.5, bf16[4,8,128,256]{3,2,1,0:T(8,128)(2,1)S(1)} %bitcast.116, bf16[4,4,128,256]{3,2,1,0:T(8,128)(2,1)} %get-tuple-element.508, ...), kind=kOutput, calls=%fused_computation.11.clone.1 | convolution fusion | flops 270532096 | bytes 4475424 | tf_op jit(solution)/shard_map/while/body/eval_jaxpr/gbd,gscd->gbsc/dot_general | solution.py:47
  73.6 0.8 exponential_reduce_fusion.2
  75.9 1.9 %select_reduce_fusion.2 = (f32[4,128]{1,0:T(4,128)S(1)}, f32[4,128,8,128]{1,3,2,0:T(8,128)S(1)}) fusion(f32[4,8,128]{2,1,0:T(8,128)S(1)} %bitcast.117, pred[4,8]{1,0:T(4,128)(4,1)S(1)} %iota_compare_fusion.5, bf16[4,8,128,256]{3,2,1,0:T(8,128)(2,1)S(1)} %bitcast.116, bf16[4,4,128,256]{3,2,1,0:T(8,128)(2,1)} %get-tuple-element.508, ...), kind=kOutput, calls=%fused_computation.11.clone.1 | convolution fusion | flops 270532096 | bytes 4475424 | tf_op jit(solution)/shard_map/while/body/eval_jaxpr/gbd,gscd->gbsc/dot_general | solution.py:47
  77.7 0.8 exponential_reduce_fusion.2
  80.0 1.9 %select_reduce_fusion.2 = (f32[4,128]{1,0:T(4,128)S(1)}, f32[4,128,8,128]{1,3,2,0:T(8,128)S(1)}) fusion(f32[4,8,128]{2,1,0:T(8,128)S(1)} %bitcast.117, pred[4,8]{1,0:T(4,128)(4,1)S(1)} %iota_compare_fusion.5, bf16[4,8,128,256]{3,2,1,0:T(8,128)(2,1)S(1)} %bitcast.116, bf16[4,4,128,256]{3,2,1,0:T(8,128)(2,1)} %get-tuple-element.508, ...), kind=kOutput, calls=%fused_computation.11.clone.1 | convolution fusion | flops 270532096 | bytes 4475424 | tf_op jit(solution)/shard_map/while/body/eval_jaxpr/gbd,gscd->gbsc/dot_general | solution.py:47
  81.9 0.8 exponential_reduce_fusion.2
  84.1 1.9 %select_reduce_fusion.2 = (f32[4,128]{1,0:T(4,128)S(1)}, f32[4,128,8,128]{1,3,2,0:T(8,128)S(1)}) fusion(f32[4,8,128]{2,1,0:T(8,128)S(1)} %bitcast.117, pred[4,8]{1,0:T(4,128)(4,1)S(1)} %iota_compare_fusion.5, bf16[4,8,128,256]{3,2,1,0:T(8,128)(2,1)S(1)} %bitcast.116, bf16[4,4,128,256]{3,2,1,0:T(8,128)(2,1)} %get-tuple-element.508, ...), kind=kOutput, calls=%fused_computation.11.clone.1 | convolution fusion | flops 270532096 | bytes 4475424 | tf_op jit(solution)/shard_map/while/body/eval_jaxpr/gbd,gscd->gbsc/dot_general | solution.py:47
  86.0 0.8 exponential_reduce_fusion.2
  86.8 5.2 %all-gather = f32[16,4,128]{2,1,0:T(4,128)S(1)} all-gather(f32[4,4,128]{2,1,0:T(4,128)S(1)} %get-tuple-element.235), channel_id=2, replica_groups=mesh['imp'=8,'camp'=4] {'camp'}, dimensions={0}, use_global_device_ids=true | all-gather | bytes 40960 | tf_op jit(solution)/shard_map/all_gather | solution.py:13
  92.0 5.2 %all-gather.1 = f32[16,4,128]{2,1,0:T(4,128)S(1)} all-gather(f32[4,4,128]{2,1,0:T(4,128)S(1)} %get-tuple-element.236), channel_id=3, replica_groups=mesh['imp'=8,'camp'=4] {'camp'}, dimensions={0}, use_global_device_ids=true | all-gather | bytes 40960 | tf_op jit(solution)/shard_map/all_gather | solution.py:13
  97.3 14.7 %while.42 = (s32[]{:T(128)}, f32[8,128]{1,0:T(8,128)S(1)}, s32[4,4,8]{2,1,0:T(4,128)S(1)}, s32[4,4]{1,0:T(4,128)S(1)}, bf16[4,4,128,256]{3,2,1,0:T(8,128)(2,1)},...) while((s32[]{:T(128)}, f32[8,128]{1,0:T(8,128)S(1)}, ...), condition=%wide.region_8.9_spmd.clone, body=%wide.region_6.8_spmd.clone.sunk | while | flops 272498304 | bytes 6668323 | solution.py:84
  98.8 2.0 %multiply_reduce_fusion.2 = f32[4,8,128]{2,1,0:T(8,128)S(1)} fusion(bf16[4,8,128,256]{3,2,1,0:T(8,128)(2,1)S(1)} %bitcast.115, f32[4,128]{1,0:T(4,128)S(1)} %get-tuple-element.484, f32[4,128]{1,0:T(4,128)S(1)} %get-tuple-element.485, f32[4,128]{1,0:T(4,128)S(1)} %dynamic-slice_bitcast_fusion.8, f32[4,8,128]{2,1,0:T(8,128)S(1)} %bitcast.121, ...), kind=kOutput, calls=%fused_computation.24.clone.1 | convolution fusion | flops 272101376 | bytes 2398752 | tf_op jit(solution)/shard_map/while/body/eval_jaxpr/gbd,gscd->gbsc/dot_general | solution.py:47
  101.1 0.7 gather_fusion.2
  102.5 2.0 %multiply_reduce_fusion.2 = f32[4,8,128]{2,1,0:T(8,128)S(1)} fusion(bf16[4,8,128,256]{3,2,1,0:T(8,128)(2,1)S(1)} %bitcast.115, f32[4,128]{1,0:T(4,128)S(1)} %get-tuple-element.484, f32[4,128]{1,0:T(4,128)S(1)} %get-tuple-element.485, f32[4,128]{1,0:T(4,128)S(1)} %dynamic-slice_bitcast_fusion.8, f32[4,8,128]{2,1,0:T(8,128)S(1)} %bitcast.121, ...), kind=kOutput, calls=%fused_computation.24.clone.1 | convolution fusion | flops 272101376 | bytes 2398752 | tf_op jit(solution)/shard_map/while/body/eval_jaxpr/gbd,gscd->gbsc/dot_general | solution.py:47
  104.8 0.7 gather_fusion.2
  106.2 2.0 %multiply_reduce_fusion.2 = f32[4,8,128]{2,1,0:T(8,128)S(1)} fusion(bf16[4,8,128,256]{3,2,1,0:T(8,128)(2,1)S(1)} %bitcast.115, f32[4,128]{1,0:T(4,128)S(1)} %get-tuple-element.484, f32[4,128]{1,0:T(4,128)S(1)} %get-tuple-element.485, f32[4,128]{1,0:T(4,128)S(1)} %dynamic-slice_bitcast_fusion.8, f32[4,8,128]{2,1,0:T(8,128)S(1)} %bitcast.121, ...), kind=kOutput, calls=%fused_computation.24.clone.1 | convolution fusion | flops 272101376 | bytes 2398752 | tf_op jit(solution)/shard_map/while/body/eval_jaxpr/gbd,gscd->gbsc/dot_general | solution.py:47
  109.9 2.0 %multiply_reduce_fusion.2 = f32[4,8,128]{2,1,0:T(8,128)S(1)} fusion(bf16[4,8,128,256]{3,2,1,0:T(8,128)(2,1)S(1)} %bitcast.115, f32[4,128]{1,0:T(4,128)S(1)} %get-tuple-element.484, f32[4,128]{1,0:T(4,128)S(1)} %get-tuple-element.485, f32[4,128]{1,0:T(4,128)S(1)} %dynamic-slice_bitcast_fusion.8, f32[4,8,128]{2,1,0:T(8,128)S(1)} %bitcast.121, ...), kind=kOutput, calls=%fused_computation.24.clone.1 | convolution fusion | flops 272101376 | bytes 2398752 | tf_op jit(solution)/shard_map/while/body/eval_jaxpr/gbd,gscd->gbsc/dot_general | solution.py:47
  112.1 30.6 %all-gather.4 = f32[8,1,1024]{2,1,0:T(1,128)S(1)} all-gather(f32[1,1,1024]{2,1,0:T(1,128)S(1)} %bitcast.125), channel_id=1, replica_groups=mesh['imp'=8,'camp'=4] {'imp'}, dimensions={0}, use_global_device_ids=true | all-gather | bytes 36864 | tf_op jit(solution)/shard_map/all_gather | solution.py:89
  (98 shorter events, 14.5 us)
Async XLA Ops:
  7.2 63.1 %all-gather.7.cloned.1.call-start = ((), (), s32[]{:S(2)}) async-start(), calls=%async_computation | async-start | bytes 1310720 | tf_op jit(solution)/shard_map/all_gather | solution.py:25
  97.3 46.0 %copy-start = (bf16[128]{0:T(256)(128)(2,1)S(1)}, bf16[128]{0:T(256)(128)(2,1)}, u32[]{:S(2)}) copy-start(bf16[128]{0:T(256)(128)(2,1)} %param.16) | copy-start | bytes 772
  97.3 46.0 %copy-start.1 = (f32[128]{0:T(128)S(1)}, f32[128]{0:T(128)}, u32[]{:S(2)}) copy-start(f32[128]{0:T(128)} %param.17) | copy-start | bytes 1540
Sparse Core Ops, SparseCore 0:
  9.5 19.4 all-gather.6
